TPU v7x, 32 devices: a whole 2x2x4 slice. The times are simulated.
32 devices in a mesh: rec: 4 (over x, core), tm: 8 (over z, y).
Axes of the slice: x: 2, y: 2, z: 4, core: 2. Of those that a mesh axis runs over, the one named last changes fastest.
Arguments:
- signal: bfloat16 [8192, 1280], P(('rec', 'tm')), parts along dimension 0, may hold values from -6 to 6
- position_kernel: bfloat16 [1280, 80, 128], P('tm'), may hold values from -0.0625 to 0.0625
- position_bias: float32 [1280], P('tm'), may hold values from -3 to 3
- layer_gain: float32 [1280], replicated, may hold values from 0.5 to 1.5
- layer_shift: float32 [1280], replicated, may hold values from -3 to 3
- query_weight: bfloat16 [1280, 640], P('tm'), may hold values from -0.25 to 0.25
- query_bias: float32 [640], replicated, may hold values from -4 to 4
- key_weight: bfloat16 [1280, 640], P('tm'), may hold values from -0.25 to 0.25
- value_weight: bfloat16 [1280, 640], P('tm'), may hold values from -0.15625 to 0.15625
- value_bias: float32 [640], replicated, may hold values from -3 to 3
- output_weight: bfloat16 [640, 1280], P(None, 'tm'), may hold values from -0.25 to 0.25
- output_bias: float32 [1280], replicated, may hold values from -3 to 3
- key_blocks: int32 [64, 5], P(('rec', 'tm')), parts along dimension 0, may hold values from -1 to 15, as said below
- global_blocks: int32 [16], P('rec'), parts along dimension 0, may hold values from 0 to 15, as said below
Outputs:
- encoded: bfloat16 [8192, 1280], P(('rec', 'tm')), parts along dimension 0
There are 4 independent parts, one for each index of `rec`. A program takes and returns all parts, laid end to end along the dimension named above; an argument that names none is the same for every part. Nothing has to cross between parts.
Inputs may be any that keep to these rules, and one draw needn't show every extreme that they name: `key_blocks`: row b lists distinct blocks in any order, padded with -1; it always holds b itself, and otherwise only blocks c with |c - b| <= 2 that lie in b's segment, segments being runs of consecutive blocks of the recording. `global_blocks`: 4 distinct block numbers of the recording.
All inputs are finite; a program needn't handle non-finite values.
Results may differ from a plain program's by a relative error of at most 0.0055.
Values may be sent and summed in bfloat16 or wider, within the bound.
A program may use at most 128 MiB of HBM per device.

v0:
```python
import math

import jax
import jax.numpy as jnp
import numpy as np
from jax import lax
from jax.sharding import PartitionSpec as P

HEAD = 80
HEADS = 8
BLOCK = 128
GLOBALS = 4


EPSILON = 1e-05


def attend(queries, key_rows, value_rows, allowed):
    block_count, row_count, heads_width = queries.shape
    query_heads = queries.reshape(block_count, row_count, HEADS, HEAD)
    key_heads = key_rows.reshape(block_count, key_rows.shape[1], HEADS, HEAD)
    value_heads = value_rows.reshape(block_count, value_rows.shape[1], HEADS, HEAD)
    scores = jnp.einsum(
        "bqhe,bkhe->bhqk", query_heads, key_heads, preferred_element_type=jnp.float32
    ) * (1.0 / math.sqrt(HEAD))
    scores = jnp.where(allowed[:, None, None, :], scores, -jnp.inf)
    row_max = jnp.max(scores, axis=-1, keepdims=True)
    weights = jnp.exp(scores - row_max)
    row_total = jnp.sum(weights, axis=-1)
    probability = weights.astype(jnp.bfloat16)
    context_sum = jnp.einsum(
        "bhqk,bkhe->bqhe", probability, value_heads, preferred_element_type=jnp.float32
    )
    context = context_sum / jnp.transpose(row_total, (0, 2, 1))[..., None]
    return context.reshape(block_count, row_count, heads_width).astype(jnp.bfloat16)


def body(
    signal,
    position_kernel,
    position_bias,
    layer_gain,
    layer_shift,
    query_weight,
    query_bias,
    key_weight,
    value_weight,
    value_bias,
    output_weight,
    output_bias,
    key_blocks,
    global_blocks,
):
    devices = lax.axis_size("tm")
    frame_count, model_width = signal.shape
    channel_share, group_width, kernel_taps = position_kernel.shape
    inner_width = max(channel_share, group_width)
    folded = signal.T
    if channel_share >= group_width:
        outgoing = folded.reshape(devices, channel_share, frame_count)
    else:
        start_groups = np.arange(devices) * channel_share // group_width
        outgoing = jnp.take(
            folded.reshape(model_width // group_width, group_width, frame_count),
            start_groups,
            axis=0,
        )
    incoming = lax.all_to_all(outgoing, "tm", split_axis=0, concat_axis=2, tiled=True)
    response = lax.conv_general_dilated(
        incoming,
        position_kernel,
        (1,),
        [(kernel_taps // 2, kernel_taps // 2 - 1)],
        dimension_numbers=("NCH", "OIH", "NCH"),
        feature_group_count=inner_width // group_width,
        preferred_element_type=jnp.float32,
    )[0]
    position = jax.nn.gelu(response + position_bias[:, None], approximate=False).astype(
        jnp.bfloat16
    )
    returned = lax.all_to_all(position, "tm", split_axis=1, concat_axis=0, tiled=True)
    hidden = signal.astype(jnp.float32) + returned.T.astype(jnp.float32)
    average = jnp.mean(hidden, axis=-1, keepdims=True)
    centered = hidden - average
    variance = jnp.mean(centered * centered, axis=-1, keepdims=True)
    normed = (centered * lax.rsqrt(variance + EPSILON) * layer_gain + layer_shift).astype(
        jnp.bfloat16
    )
    heads_width = query_weight.shape[1]
    zero_sums = jnp.zeros((frame_count, heads_width), jnp.float32)
    totals = (zero_sums, zero_sums, zero_sums)
    pieces = (
        lax.all_gather(query_weight, "tm", axis=0, tiled=True),
        lax.all_gather(key_weight, "tm", axis=0, tiled=True),
        lax.all_gather(value_weight, "tm", axis=0, tiled=True),
    )
    columns = lax.slice_in_dim(normed, 0, pieces[0].shape[0], axis=1)
    query_sum, key_sum, value_sum = tuple(
        (
            running + jnp.dot(columns, weight_rows, preferred_element_type=jnp.float32)
            for running, weight_rows in zip(totals, pieces)
        )
    )
    queries = (query_sum + query_bias).astype(jnp.bfloat16)
    key_part = key_sum.astype(jnp.bfloat16)
    value_part = (value_sum + value_bias).astype(jnp.bfloat16)
    key_value = jnp.stack((key_part, value_part), axis=1)
    per_device = frame_count // BLOCK
    repeated = jnp.any(global_blocks[None, :, None] == key_blocks[:, None, :], axis=-1)
    whole = lax.all_gather(key_value, "tm", axis=0, tiled=True)
    block_ids = jnp.concatenate(
        [key_blocks, jnp.broadcast_to(global_blocks[None, :], (per_device, GLOBALS))], axis=1
    )
    allowed = jnp.concatenate([key_blocks >= 0, jnp.logical_not(repeated)], axis=1)
    candidates = whole.reshape(-1, BLOCK, 2, heads_width)[jnp.maximum(block_ids, 0)]
    key_rows = candidates[:, :, :, 0].reshape(per_device, -1, heads_width)
    value_rows = candidates[:, :, :, 1].reshape(per_device, -1, heads_width)
    allowed_rows = jnp.repeat(allowed, BLOCK, axis=1)
    context = attend(
        queries.reshape(per_device, BLOCK, heads_width), key_rows, value_rows, allowed_rows
    ).reshape(frame_count, heads_width)
    projected = jnp.dot(
        context,
        lax.all_gather(output_weight, "tm", axis=1, tiled=True),
        preferred_element_type=jnp.float32,
    )
    return (hidden + projected + output_bias).astype(jnp.bfloat16)


def solution(mesh):
    placed = (
        P(("rec", "tm"), None),
        P("tm", None, None),
        P("tm"),
        P(),
        P(),
        P("tm", None),
        P(),
        P("tm", None),
        P("tm", None),
        P(),
        P(None, "tm"),
        P(),
        P(("rec", "tm"), None),
        P("rec"),
    )
    return jax.shard_map(
        body, mesh=mesh, in_specs=placed, out_specs=P(("rec", "tm"), None), check_vma=False
    )
```

profile of v0, /device:TPU:0, one launch (start us, length us, event | category | flops | bytes accessed | tf_op | source)
XLA Modules:
  0.0 464.3 jit_solution(16958150872306286310)
XLA Ops:
  6.5 0.7 all-gather.6.cloned.1.call-update
  7.3 2.2 copy.47
  9.4 7.3 %all-to-all-start = ((bf16[8,160,256]{2,1,0:T(8,128)(2,1)}), bf16[8,160,256]{2,1,0:T(8,128)(2,1)S(1)}, u32[]{:S(2)}, u32[]{:S(2)}) async-start(bf16[8,160,256]{2,1,0:T(8,128)(2,1)} %bitcast.1), calls=%async_computation | async-start | bytes 1310720 | tf_op jit(solution)/shard_map/all_to_all | solution.py:68
  16.7 0.7 all-gather.8.cloned.1.call-update
  17.5 7.9 %copy.50 = bf16[2,80,80,128]{2,1,0,3:T(8,128)(2,1)} copy(bf16[2,80,80,128]{3,2,1,0:T(8,128)(2,1)} %bitcast.80) | data formatting | bytes 6553600 | tf_op jit(solution)/shard_map/shard_map
  25.4 15.2 %all-to-all-done = bf16[8,160,256]{2,1,0:T(8,128)(2,1)S(1)} async-done(((bf16[8,160,256]{2,1,0:T(8,128)(2,1)}), bf16[8,160,256]{2,1,0:T(8,128)(2,1)S(1)}, u32[]{:S(2)}, u32[]{:S(2)}) %all-to-all-start) | async-done | bytes 655392 | tf_op jit(solution)/shard_map/all_to_all | solution.py:68
  41.1 1.1 reshape.94
  42.2 217.4 %fusion.50 = f32[1,2,80,2048]{2,0,1,3:T(1,128)} fusion(bf16[1,2,80,2048]{2,0,1,3:T(2,128)(2,1)S(1)} %reshape.94, bf16[2,80,80,128]{2,1,0,3:T(8,128)(2,1)} %copy.50), kind=kOutput, calls=%fused_computation.67 | convolution fusion | flops 6606028800 | bytes 5242880 | tf_op jit(solution)/shard_map/conv_general_dilated | solution.py:69
  259.6 4.5 copy.51
  264.8 3.5 fusion.16
  268.3 1.0 copy.52
  269.3 3.5 all-to-all-start.1
  272.9 0.7 all-gather.12.cloned.1.call-update
  273.6 19.1 %all-to-all-done.1 = bf16[160,8,256]{2,0,1:T(8,128)(2,1)S(1)} async-done(((bf16[160,8,256]{2,0,1:T(8,128)(2,1)}), bf16[160,8,256]{2,0,1:T(8,128)(2,1)S(1)}, u32[]{:S(2)}, u32[]{:S(2)}) %all-to-all-start.1) | async-done | bytes 655392 | tf_op jit(solution)/shard_map/all_to_all | solution.py:81
  293.2 0.7 copy-done
  295.1 2.1 fusion.32
  297.3 2.1 fusion.31
  299.5 0.9 pad_maximum_fusion
  301.6 20.9 %all-gather.12.cloned.1.call-done = bf16[1280,640]{1,0:T(8,128)(2,1)} async-done(((bf16[160,640]{1,0:T(8,128)(2,1)}), bf16[1280,640]{1,0:T(8,128)(2,1)}) %all-gather.12.cloned.1.call-update) | async-done | bytes 1638416 | tf_op jit(solution)/shard_map/all_gather | solution.py:93
  322.5 2.1 fusion.30
  324.6 0.6 reshape.95
  325.2 84.5 %all-gather.10.cloned.1.call-done = bf16[2048,2,640]{2,0,1:T(8,128)(2,1)} async-done(((bf16[256,2,640]{2,0,1:T(8,128)(2,1)}), bf16[2048,2,640]{2,0,1:T(8,128)(2,1)}) %all-gather.10.cloned.1.call-update) | async-done | bytes 5242896 | tf_op jit(solution)/shard_map/all_gather | solution.py:110
  409.7 7.4 %gather_fusion = bf16[18,128,2,640]{3,1,2,0:T(8,128)(2,1)} fusion(bf16[16,128,2,640]{3,1,0,2:T(8,128)(2,1)} %bitcast.77, s32[1024]{0:T(1024)S(1)} %pad_clamp_fusion), kind=kCustom, calls=%fused_computation | custom fusion | bytes 11796552 | tf_op jit(solution)/shard_map/gather | solution.py:115
  417.2 3.5 copy.54
  420.7 3.2 fusion.49
  423.9 8.6 %reshape_reshape_squeeze.7 = bf16[2,1152,8,80]{3,2,1,0:T(8,128)(2,1)} reshape(bf16[2,9,128,1,640]{4,2,1,0,3:T(8,128)(2,1)} %get-tuple-element.6) | data formatting | bytes 5898240 | tf_op jit(solution)/shard_map/reshape;reshape;squeeze | solution.py:21
  432.5 8.7 %reshape_reshape_squeeze.6 = bf16[2,1152,8,80]{3,2,1,0:T(8,128)(2,1)} reshape(bf16[2,9,128,1,640]{4,2,1,0,3:T(8,128)(2,1)} %get-tuple-element.5) | data formatting | bytes 5898240 | tf_op jit(solution)/shard_map/reshape;reshape;squeeze | solution.py:22
  441.2 4.6 fusion
  445.8 2.2 fusion.1
  448.0 5.3 %fusion.38 = bf16[2,128,8,80]{1,3,2,0:T(8,128)(2,1)S(1)} fusion(f32[2,8,128,1152]{3,2,1,0:T(8,128)S(1)} %get-tuple-element.8, f32[2,8,128]{2,1,0:T(8,128)S(1)} %get-tuple-element.7, pred[2,1152]{1,0:T(4,128)(4,1)S(1)} %bitcast.85, bf16[2,1152,8,80]{3,2,1,0:T(8,128)(2,1)} %reshape_reshape_squeeze.6, f32[2,128,8]{1,2,0:T(8,128)S(1)} %bitcast.86), kind=kOutput, calls=%fused_computation.49 | convolution fusion | flops 387252224 | bytes 12732672 | tf_op jit(solution)/shard_map/bhqk,bkhe->bqhe/dot_general | solution.py:31
  453.6 0.9 all-gather.14.cloned.1.call-done
  454.5 3.0 fusion.13
  (46 shorter events, 4.6 us)
Async XLA Ops:
  6.5 288.6 %all-gather.6.cloned.1.call-start = ((), (), s32[]{:S(2)}) async-start(), calls=%async_computation.2 | async-start | bytes 1843200 | tf_op jit(solution)/shard_map/all_gather | solution.py:94
  9.4 31.2 %all-to-all-start = ((bf16[8,160,256]{2,1,0:T(8,128)(2,1)}), bf16[8,160,256]{2,1,0:T(8,128)(2,1)S(1)}, u32[]{:S(2)}, u32[]{:S(2)}) async-start(bf16[8,160,256]{2,1,0:T(8,128)(2,1)} %bitcast.1), calls=%async_computation | async-start | bytes 1310720 | tf_op jit(solution)/shard_map/all_to_all | solution.py:68
  16.7 280.6 %all-gather.8.cloned.1.call-start = ((), (), s32[]{:S(2)}) async-start(), calls=%async_computation.3 | async-start | bytes 1843200 | tf_op jit(solution)/shard_map/all_gather | solution.py:95
  264.1 0.7 copy-start.5
  269.3 23.4 %all-to-all-start.1 = ((bf16[160,8,256]{2,0,1:T(8,128)(2,1)}), bf16[160,8,256]{2,0,1:T(8,128)(2,1)S(1)}, u32[]{:S(2)}, u32[]{:S(2)}) async-start(bf16[160,8,256]{2,0,1:T(8,128)(2,1)} %copy.52), calls=%async_computation.1 | async-start | bytes 1310720 | tf_op jit(solution)/shard_map/all_to_all | solution.py:81
  272.8 49.7 %all-gather.12.cloned.1.call-start = ((), (), s32[]{:S(2)}) async-start(), calls=%async_computation.5 | async-start | bytes 1843200 | tf_op jit(solution)/shard_map/all_gather | solution.py:93
  273.5 136.2 %all-gather.10.cloned.1.call-start = ((), (), s32[]{:S(2)}) async-start(), calls=%async_computation.4 | async-start | bytes 5898240 | tf_op jit(solution)/shard_map/all_gather | solution.py:110
  292.8 1.1 copy-start
  294.1 0.7 copy-start.1
  294.1 0.7 copy-start.2
  295.1 2.2 copy-start.7
  299.4 1.6 copy-start.4
  299.4 1.6 copy-start.6
  299.5 23.0 %copy-start.8 = (f32[640]{0:T(1024)S(1)}, f32[640]{0:T(1024)}, u32[]{:S(2)}) copy-start(f32[640]{0:T(1024)} %param.20) | copy-start | bytes 7684
  300.4 154.1 %all-gather.14.cloned.1.call-start = ((), (), s32[]{:S(2)}) async-start(), calls=%async_computation.6 | async-start | bytes 1843200 | tf_op jit(solution)/shard_map/all_gather | solution.py:124
  448.0 6.5 %copy-start.3 = (f32[1280]{0:T(1024)S(1)}, f32[1280]{0:T(1024)}, u32[]{:S(2)}) copy-start(f32[1280]{0:T(1024)} %param.25) | copy-start | bytes 15364
Sparse Core Ops, SparseCore 0:
  9.5 53.3 all-gather.5
  65.1 43.3 all-gather.7
  275.8 46.6 all-gather.11
  324.5 85.1 all-gather.9
  411.7 42.7 all-gather.13
where the time goes:
time: 466 us; the launch traced here: 464 us
  matrix products  237 us (51%)
  waiting for transfers between devices  143 us (31%)
  local copies, waits for them, and re-layouts  51.9 us (11%)
  between operations  13.7 us (3%)
  starting transfers between devices  11 us (2%)
  other arithmetic  7.86 us (2%)
    conv_general_dilated x1, matrix products, body(): lax.conv_general_dilated(incoming, position_kernel, (1,), [(kernel_taps /...  217 us
    all_gather x1, waiting for transfers between devices, body(): whole = lax.all_gather(key_value, 'tm', axis=0, tiled=True)  84.5 us
    all_gather x1, waiting for transfers between devices, body(): lax.all_gather(query_weight, 'tm', axis=0, tiled=True)  20.9 us
    all_to_all x1, waiting for transfers between devices, body(): lax.all_to_all(position, 'tm', split_axis=1, concat_axis=0, tiled=True)  19.1 us
    all_to_all x1, waiting for transfers between devices, body(): lax.all_to_all(outgoing, 'tm', split_axis=0, concat_axis=2, tiled=True)  15.2 us
    gather x2, local copies, waits for them, and re-layouts, body(): whole.reshape(-1, BLOCK, 2, heads_width)[jnp.maximum(block_ids, 0)]  10.9 us
  transfers between devices with their start and end apart: 7, of which 5 were waited for; matrix products, arithmetic and copies ran while one was open for 63% of the time, Pallas kernels for 0%

commit v1 on v0

--- a/solution.py
+++ b/solution.py
@@ -4,6 +4,8 @@
 import jax.numpy as jnp
 import numpy as np
 from jax import lax
+from jax.experimental import pallas as pl
+from jax.experimental.pallas import tpu as pltpu
 from jax.sharding import PartitionSpec as P
 
 HEAD = 80
@@ -35,7 +37,7 @@
     return context.reshape(block_count, row_count, heads_width).astype(jnp.bfloat16)
 
 
-def body(
+def general(
     signal,
     position_kernel,
     position_bias,
@@ -127,6 +129,194 @@
     return (hidden + projected + output_bias).astype(jnp.bfloat16)
 
 
+PHASES = 3
+LANES = 256
+STEP = 4
+
+
+def conv_kernel(rows, steps, x_ref, w_ref, o_ref):
+    o_ref[0] = jnp.zeros_like(o_ref[0])
+
+    for step in range(0, steps, STEP):
+        window = jnp.concatenate(
+            [
+                x_ref[0, step + at : step + at + rows, :].astype(jnp.bfloat16)
+                for at in range(STEP)
+            ],
+            axis=1,
+        )
+        taps = w_ref[0, step : step + STEP].reshape(STEP * LANES, LANES)
+        o_ref[0] += jnp.dot(window, taps, preferred_element_type=jnp.float32)
+
+
+def position_term(incoming, position_kernel, position_bias):
+    frames, channels = incoming.shape
+    _, width, taps = position_kernel.shape
+    groups = channels // width
+    reach = taps // 2
+    lead = -(-reach // PHASES)
+    shift = lead * PHASES - reach
+    steps = -(-(taps + shift + PHASES - 1) // (PHASES * STEP)) * STEP
+    rows = -(-frames // PHASES)
+    rows_padded = -(-rows // 16) * 16
+    total_rows = -(-(rows_padded + steps) // 8) * 8
+    front = lead * PHASES
+    inner = PHASES * width
+    spread = jnp.pad(incoming, ((front, total_rows * PHASES - front - frames), (0, 0)))
+    spread = spread.reshape(total_rows, PHASES, groups, width)
+    spread = spread.transpose(2, 0, 1, 3).reshape(groups, total_rows, inner)
+    spread = jnp.pad(spread, ((0, 0), (0, 0), (0, LANES - inner))).astype(jnp.float32)
+    kernels = position_kernel.reshape(groups, width, width, taps).transpose(0, 3, 2, 1)
+    span = steps * PHASES
+    matrix = jnp.concatenate(
+        [
+            jnp.pad(
+                kernels,
+                ((0, 0), (shift + phase, span - taps - shift - phase), (0, 0), (0, 0)),
+            )
+            for phase in range(PHASES)
+        ],
+        axis=3,
+    ).reshape(groups, steps, inner, inner)
+    matrix = jnp.pad(matrix, ((0, 0), (0, 0), (0, LANES - inner), (0, LANES - inner)))
+    response = pl.pallas_call(
+        lambda *refs: conv_kernel(rows_padded, steps, *refs),
+        out_shape=jax.ShapeDtypeStruct((groups, rows_padded, LANES), jnp.float32),
+        grid=(groups,),
+        in_specs=[
+            pl.BlockSpec((1, total_rows, LANES), lambda g: (g, 0, 0)),
+            pl.BlockSpec((1, steps, LANES, LANES), lambda g: (g, 0, 0, 0)),
+        ],
+        out_specs=pl.BlockSpec((1, rows_padded, LANES), lambda g: (g, 0, 0)),
+        compiler_params=pltpu.CompilerParams(vmem_limit_bytes=40 * 1024 * 1024),
+    )(spread, matrix)
+    biases = jnp.tile(position_bias.reshape(groups, 1, width), (1, 1, PHASES))
+    position = jax.nn.gelu(response[:, :rows, :inner] + biases, approximate=False)
+    position = position.astype(jnp.bfloat16).reshape(groups, rows * PHASES, width)
+    return position[:, :frames].transpose(1, 0, 2).reshape(frames, channels)
+
+
+def attention_kernel(listed, scale, ids_ref, mask_ref, q_ref, k_ref, v_ref, o_ref):
+    row = pl.program_id(0)
+    queries = q_ref[...]
+    scores, values = [], []
+    for at in range(listed):
+        begin = pl.multiple_of(ids_ref[row, at] * BLOCK, BLOCK)
+        score = lax.dot_general(
+            queries,
+            k_ref[pl.ds(begin, BLOCK), :],
+            (((1,), (1,)), ((), ())),
+            preferred_element_type=jnp.float32,
+        )
+        scores.append(jnp.where(mask_ref[row, at] > 0, score * scale, -jnp.inf))
+        values.append(v_ref[pl.ds(begin, BLOCK), :])
+    peak = scores[0]
+    for score in scores[1:]:
+        peak = jnp.maximum(peak, score)
+    peak = jnp.max(peak, axis=1, keepdims=True)
+    weights = [jnp.exp(score - peak) for score in scores]
+    total = weights[0]
+    for weight in weights[1:]:
+        total = total + weight
+    total = jnp.sum(total, axis=1, keepdims=True)
+    probability = jnp.concatenate([weight.astype(jnp.bfloat16) for weight in weights], axis=1)
+    context = jnp.dot(
+        probability, jnp.concatenate(values, axis=0), preferred_element_type=jnp.float32
+    )
+    o_ref[...] = (context / total).astype(jnp.bfloat16)
+
+
+def attend_head(queries, keys, values, block_ids, allowed):
+    frames, width = queries.shape
+    blocks, listed = block_ids.shape
+    whole = pl.BlockSpec((frames, width), lambda b, *_: (0, 0))
+    tile = pl.BlockSpec((BLOCK, width), lambda b, *_: (b, 0))
+    return pl.pallas_call(
+        lambda *refs: attention_kernel(listed, 1.0 / math.sqrt(HEAD), *refs),
+        out_shape=jax.ShapeDtypeStruct((frames, width), jnp.bfloat16),
+        grid_spec=pltpu.PrefetchScalarGridSpec(
+            num_scalar_prefetch=2,
+            grid=(blocks,),
+            in_specs=[tile, whole, whole],
+            out_specs=tile,
+        ),
+    )(block_ids, allowed, queries, keys, values)
+
+
+def by_heads(
+    signal,
+    position_kernel,
+    position_bias,
+    layer_gain,
+    layer_shift,
+    query_weight,
+    query_bias,
+    key_weight,
+    value_weight,
+    value_bias,
+    output_weight,
+    output_bias,
+    key_blocks,
+    global_blocks,
+):
+    records = lax.axis_size("rec")
+    record = lax.axis_index("rec")
+    share = query_weight.shape[0]
+    part = share // records
+    inner = HEADS * HEAD
+    stacked = jnp.stack((query_weight, key_weight, value_weight), axis=1)
+    stacked = stacked.reshape(share, 3, HEADS, HEAD).transpose(0, 2, 1, 3)
+    stacked = jnp.concatenate((stacked.reshape(share, 3 * inner), output_weight.T), axis=1)
+    mine = lax.dynamic_slice_in_dim(stacked, record * part, part, axis=0)
+
+    incoming = lax.all_to_all(signal, "tm", split_axis=1, concat_axis=0, tiled=True)
+    weights = lax.all_gather(mine, ("tm", "rec"), axis=0, tiled=True)
+    listed = lax.all_gather(key_blocks, "tm", axis=0, tiled=True)
+    position = position_term(incoming, position_kernel, position_bias)
+    returned = lax.all_to_all(position, "tm", split_axis=0, concat_axis=1, tiled=True)
+    hidden = signal.astype(jnp.float32) + returned.astype(jnp.float32)
+    average = jnp.mean(hidden, axis=-1, keepdims=True)
+    centered = hidden - average
+    variance = jnp.mean(centered * centered, axis=-1, keepdims=True)
+    normed = (centered * lax.rsqrt(variance + EPSILON) * layer_gain + layer_shift).astype(
+        jnp.bfloat16
+    )
+    biases = jnp.stack((query_bias, jnp.zeros_like(query_bias), value_bias))
+    biases = biases.reshape(3, HEADS, HEAD).transpose(1, 0, 2).reshape(-1)
+    projected = jnp.dot(normed, weights[:, : 3 * inner], preferred_element_type=jnp.float32)
+    projected = (projected + biases).astype(jnp.bfloat16)
+    headed = lax.all_to_all(projected, "tm", split_axis=1, concat_axis=0, tiled=True)
+    blocks = listed.shape[0]
+    repeated = jnp.any(global_blocks[None, :, None] == listed[:, None, :], axis=-1)
+    block_ids = jnp.concatenate(
+        [jnp.maximum(listed, 0), jnp.broadcast_to(global_blocks[None, :], (blocks, GLOBALS))],
+        axis=1,
+    )
+    allowed = jnp.concatenate([listed >= 0, jnp.logical_not(repeated)], axis=1)
+    context = attend_head(
+        headed[:, :HEAD],
+        headed[:, HEAD : 2 * HEAD],
+        headed[:, 2 * HEAD :],
+        block_ids,
+        allowed.astype(jnp.int32),
+    )
+    context = lax.all_to_all(context, "tm", split_axis=0, concat_axis=1, tiled=True)
+    projected = lax.dot_general(
+        context,
+        weights[:, 3 * inner :],
+        (((1,), (1,)), ((), ())),
+        preferred_element_type=jnp.float32,
+    )
+    return (hidden + projected + output_bias).astype(jnp.bfloat16)
+
+
+def body(*operands):
+    share, width, _ = operands[1].shape
+    fits = lax.axis_size("tm") == HEADS and share % width == 0
+    fits = fits and operands[5].shape[0] % lax.axis_size("rec") == 0
+    return (by_heads if fits else general)(*operands)
+
+
 def solution(mesh):
     placed = (
         P(("rec", "tm"), None),

time: 466 us -> 189 us (0.41)
  matrix products: 237 us -> 7.14 us
  waiting for transfers between devices: 143 us -> 23.7 us
  blocking collectives: 0 us -> 45.2 us
  Pallas kernels: 0 us -> 23 us
  local copies, waits for them, and re-layouts: 51.9 us -> 39.3 us
  other arithmetic: 7.86 us -> 18.3 us
  starting transfers between devices: 11 us -> 17.1 us
    conv_general_dilated x1 -> x0, matrix products: 217 us -> none  [body(): lax.conv_general_dilated(incoming, position_kernel, (1,), [(kernel_taps /...]
    all_gather x5 -> x1, waiting for transfers between devices: 106 us -> 0.02 us  [by_heads(): weights = lax.all_gather(mine, ('tm', 'rec'), axis=0, tiled=True)]
    all_gather x0 -> x1, blocking collectives: none -> 31.2 us  [by_heads(): listed = lax.all_gather(key_blocks, 'tm', axis=0, tiled=True)]
    pallas_call x0 -> x2, Pallas kernels: none -> 23 us  [the longest x1 14.6 us: attend_head(): pl.pallas_call(lambda *refs: attention_kernel(listed, 1.0 / math.sqrt(HEA...]
    another operation x4 -> x9, local copies, waits for them, and re-layouts: 25.8 us -> 3.75 us  [the longest x3 3.34 us: by_heads(): stacked = jnp.stack((query_weight, key_weight, value_weight), axis=1)]
    all_to_all x0 -> x1, blocking collectives: none -> 14 us  [by_heads(): lax.all_to_all(context, 'tm', split_axis=0, concat_axis=1, tiled=True)]
    concatenate x1 -> x3, other arithmetic: 0.08 us -> 13.4 us  [the longest x1 11.6 us: position_term(): jnp.concatenate([jnp.pad(kernels, ((0, 0), (shift + phase, span - taps -...]
    dot_general x6 -> x2, matrix products: 19.2 us -> 7.14 us  [the longest x1 4.12 us: by_heads(): jnp.dot(normed, weights[:, :3 * inner], preferred_element_type=jnp.float32)]
  transfers between devices with their start and end apart: 7 -> 4, of which waited for: 5 -> 1; matrix products, arithmetic and copies ran while one was open for 63% -> 22% of each run, Pallas kernels for 0% -> 4%
where the time goes in v1:
time: 189 us; the launch traced here: 187 us
  blocking collectives  45.2 us (24%)
  local copies, waits for them, and re-layouts  39.3 us (21%)
  waiting for transfers between devices  23.7 us (13%)
  Pallas kernels  23 us (12%)
  other arithmetic  18.3 us (10%)
  starting transfers between devices  17.1 us (9%)
  between operations  13.7 us (7%)
  matrix products  7.14 us (4%)
    all_gather x1, blocking collectives, by_heads(): listed = lax.all_gather(key_blocks, 'tm', axis=0, tiled=True)  31.2 us
    all_to_all x1, waiting for transfers between devices, by_heads(): lax.all_to_all(position, 'tm', split_axis=0, concat_axis=1, tiled=True)  23.6 us
    pallas_call x1, Pallas kernels, attend_head(): pl.pallas_call(lambda *refs: attention_kernel(listed, 1.0 / math.sqrt(HEA...  14.6 us
    all_to_all x1, blocking collectives, by_heads(): lax.all_to_all(context, 'tm', split_axis=0, concat_axis=1, tiled=True)  14 us
    concatenate x1, other arithmetic, position_term(): jnp.concatenate([jnp.pad(kernels, ((0, 0), (shift + phase, span - taps -...  11.6 us
    reshape x1, local copies, waits for them, and re-layouts, position_term(): position_kernel.reshape(groups, width, width, taps).transpose(0, 3, 2, 1)  8.65 us
    pallas_call x1, Pallas kernels, position_term(): pl.pallas_call(lambda *refs: conv_kernel(rows_padded, steps, *refs), out_...  8.34 us
    unnamed x29, local copies, waits for them, and re-layouts  7.6 us
  transfers between devices with their start and end apart: 4, of which 1 were waited for; matrix products, arithmetic and copies ran while one was open for 22% of the time, Pallas kernels for 4%

profile of v1, /device:TPU:0, one launch (start us, length us, event | category | flops | bytes accessed | tf_op | source)
XLA Modules:
  0.0 187.3 jit_solution(7427692009912173342)
XLA Ops:
  6.5 1.1 copy.88
  7.7 1.1 copy.89
  8.8 1.1 copy.90
  10.3 1.2 fusion.27
  11.5 0.9 copy.84
  12.5 1.1 copy.69
  13.5 7.3 %all-to-all-start = ((bf16[256,8,160]{0,2,1:T(8,128)(2,1)}), bf16[256,8,160]{0,2,1:T(8,128)(2,1)S(1)}, u32[]{:S(2)}, u32[]{:S(2)}) async-start(bf16[256,8,160]{0,2,1:T(8,128)(2,1)} %bitcast), calls=%async_computation | async-start | bytes 1310720 | tf_op jit(solution)/shard_map/all_to_all | solution.py:272
  20.8 8.7 %copy.74 = bf16[2,80,80,128]{1,2,3,0:T(8,128)(2,1)} copy(bf16[2,80,80,128]{3,2,1,0:T(8,128)(2,1)} %bitcast.47) | data formatting | bytes 6553600 | tf_op jit(solution)/shard_map/reshape | solution.py:169
  29.7 11.6 %fusion.5 = bf16[2,132,80,240]{3,2,1,0:T(8,128)(2,1)S(1)} fusion(bf16[2,128,80,80]{3,2,1,0:T(8,128)(2,1)} %bitcast.39), kind=kLoop, calls=%fused_computation.9 | loop fusion | flops 70963200 | bytes 13414400 | tf_op jit(solution)/shard_map/concatenate | solution.py:171
  41.3 5.6 %pad.29.refs_1_ = bf16[2,44,256,256]{3,2,1,0:T(8,128)(2,1)} pad(bf16[2,44,240,240]{3,2,1,0:T(8,128)(2,1)S(1)} %bitcast.38, bf16[]{:T(256)} %constant.38.clone.1), padding=0_0x0_0x0_16x0_16 | pad | bytes 21671938 | tf_op jit(solution)/shard_map/jit(_pad)/pad | solution.py:181
  47.7 0.6 reshape.72
  48.4 2.5 %copy.72 = bf16[2,736,3,80]{1,3,2,0:T(8,128)(2,1)S(1)} copy(bf16[2,736,3,80]{3,0,2,1:T(2,128)(2,1)S(1)} %bitcast.42) | data formatting | bytes 1413120 | tf_op jit(solution)/shard_map/transpose | solution.py:167
  51.3 4.3 %copy-done = bf16[2,44,256,256]{3,2,1,0:T(8,128)(2,1)S(1)} copy-done((bf16[2,44,256,256]{3,2,1,0:T(8,128)(2,1)S(1)}, bf16[2,44,256,256]{3,2,1,0:T(8,128)(2,1)}, u32[]{:S(2)}) %copy-start) | copy-done | bytes 11534360
  55.6 8.3 %shard_map.136 = f32[2,688,256]{2,1,0:T(8,128)S(1)} custom-call(f32[2,736,256]{2,1,0:T(8,128)S(1)} %pad_convert_fusion.refs_0_, bf16[2,44,256,256]{3,2,1,0:T(8,128)(2,1)S(1)} %copy-done), custom_call_target="tpu_custom_call" | custom-call | tf_op jit(solution)/shard_map/pallas_call | solution.py:182
  63.9 3.1 %fusion.19 = bf16[2,683,240]{2,1,0:T(8,128)(2,1)S(1)} fusion(f32[2,688,256]{2,1,0:T(8,128)S(1)} %shard_map.136, f32[2,240]{1,0:T(2,128)S(1)} %tile.12), kind=kLoop, calls=%fused_computation.21 | loop fusion | flops 21637440 | bytes 1968960 | tf_op jit(solution)/shard_map/convert_element_type | solution.py:195
  67.1 1.3 reshape.76
  69.1 1.0 copy.76
  70.1 6.0 %all-to-all-start.1 = ((bf16[8,256,160]{1,2,0:T(8,128)(2,1)}), bf16[8,256,160]{1,2,0:T(8,128)(2,1)S(1)}, u32[]{:S(2)}, u32[]{:S(2)}) async-start(bf16[8,256,160]{1,2,0:T(8,128)(2,1)} %copy.76), calls=%async_computation.1 | async-start | bytes 1310720 | tf_op jit(solution)/shard_map/all_to_all | solution.py:276
  76.5 23.6 %all-to-all-done.1 = bf16[8,256,160]{1,2,0:T(8,128)(2,1)S(1)} async-done(((bf16[8,256,160]{1,2,0:T(8,128)(2,1)}), bf16[8,256,160]{1,2,0:T(8,128)(2,1)S(1)}, u32[]{:S(2)}, u32[]{:S(2)}) %all-to-all-start.1) | async-done | bytes 655392 | tf_op jit(solution)/shard_map/all_to_all | solution.py:276
  101.6 4.1 %fusion.12 = bf16[256,1920]{1,0:T(8,128)(2,1)S(1)} fusion(bf16[1280,2560]{1,0:T(8,128)(2,1)} %all-gather.3.cloned.1.call-done, f32[1920]{0:T(1024)S(1)} %add.74, f32[1280]{0:T(1024)S(1)} %copy-done.10, f32[1280]{0:T(1024)S(1)} %copy-done.11, f32[256]{0:T(256)S(1)} %add_rsqrt_fusion, f32[256]{0:T(256)S(1)} %broadcast_multiply_fusion, ...), kind=kOutput, calls=%fused_computation.15 | convolution fusion | flops 1261568000 | bytes 7884288 | tf_op jit(solution)/shard_map/dot_general | solution.py:286
  105.7 1.3 copy.85
  107.0 3.8 %all-to-all-start.2 = ((bf16[256,8,240]{0,2,1:T(8,128)(2,1)}), bf16[256,8,240]{0,2,1:T(8,128)(2,1)S(1)}, u32[]{:S(2)}, u32[]{:S(2)}) async-start(bf16[256,8,240]{0,2,1:T(8,128)(2,1)} %bitcast.45), calls=%async_computation.2 | async-start | bytes 1966080 | tf_op jit(solution)/shard_map/all_to_all | solution.py:288
  110.8 31.2 %all-gather = s32[8,2,5]{2,1,0:T(2,128)S(1)} all-gather(s32[1,2,5]{2,1,0:T(2,128)S(1)} %bitcast.61), channel_id=1, replica_groups=mesh['rec'=4,'tm'=8] {'tm'}, dimensions={0}, use_global_device_ids=true | all-gather | bytes 360 | tf_op jit(solution)/shard_map/all_gather | solution.py:274
  142.3 0.7 add_convert_fusion.2.refs_1_
  143.0 0.6 pad_add_fusion.refs_0_
  143.6 0.9 copy-done.2
  144.6 1.5 copy.86
  146.0 1.5 fusion.33
  147.6 14.6 %shard_map.137 = bf16[2048,80]{1,0:T(8,128)(2,1)} custom-call(s32[16,9]{1,0:T(8,128)} %pad_add_fusion.refs_0_, s32[16,9]{1,0:T(8,128)} %add_convert_fusion.2.refs_1_, bf16[2048,80]{1,0:T(8,128)(2,1)} %get-tuple-element.7.refs_2_, bf16[2048,80]{1,0:T(8,128)(2,1)} %get-tuple-element.6.refs_3_, bf16[2048,80]{1,0:T(8,128)(2,1)} %get-tuple-element.5.refs_4_), custom_call_target="tpu_custom_call" | custom-call | tf_op jit(solution)/shard_map/pallas_call | solution.py:234
  162.2 1.2 copy.87
  163.4 14.0 %all_to_all.70 = bf16[8,256,80]{1,2,0:T(8,128)(2,1)S(1)} all-to-all(bf16[8,256,80]{1,2,0:T(8,128)(2,1)S(1)} %copy.87), channel_id=1, replica_groups=mesh['rec'=4,'tm'=8] {'tm'}, dimensions={0} | all-to-all | bytes 655360 | tf_op jit(solution)/shard_map/all_to_all | solution.py:303
  177.4 3.0 %fusion.15 = bf16[256,1280]{1,0:T(8,128)(2,1)} fusion(bf16[256,640]{0,1:T(8,128)(2,1)S(1)} %bitcast.53, bf16[1280,2560]{1,0:T(8,128)(2,1)} %all-gather.3.cloned.1.call-done, f32[1280]{0:T(1024)S(1)} %copy-done.4, f32[256,1280]{1,0:T(8,128)S(1)} %copy.77, bf16[256,1280]{1,0:T(8,128)(2,1)S(1)} %copy-done.1), kind=kOutput, calls=%fused_computation.16 | convolution fusion | flops 421068800 | bytes 4592640 | tf_op jit(solution)/shard_map/dot_general | solution.py:304
  (57 shorter events, 4.7 us)
Async XLA Ops:
  6.5 3.4 %copy-start.3 = (bf16[640,160]{0,1:T(8,128)(2,1)S(1)}, bf16[640,160]{0,1:T(8,128)(2,1)}, u32[]{:S(2)}) copy-start(bf16[640,160]{0,1:T(8,128)(2,1)} %param.24) | copy-start | bytes 614404
  6.5 94.7 %all-gather.3.cloned.1.call-start = ((), (), s32[]{:S(2)}) async-start(), calls=%async_computation.4 | async-start | bytes 6758400 | tf_op jit(solution)/shard_map/all_gather | solution.py:273
  10.3 2.2 %copy-start.1 = (bf16[256,1280]{1,0:T(8,128)(2,1)S(1)}, bf16[256,1280]{1,0:T(8,128)(2,1)}, u32[]{:S(2)}) copy-start(bf16[256,1280]{1,0:T(8,128)(2,1)} %param.14) | copy-start | bytes 1966084
  13.5 33.4 %all-to-all-start = ((bf16[256,8,160]{0,2,1:T(8,128)(2,1)}), bf16[256,8,160]{0,2,1:T(8,128)(2,1)S(1)}, u32[]{:S(2)}, u32[]{:S(2)}) async-start(bf16[256,8,160]{0,2,1:T(8,128)(2,1)} %bitcast), calls=%async_computation | async-start | bytes 1310720 | tf_op jit(solution)/shard_map/all_to_all | solution.py:272
  20.8 8.7 %copy-start.8 = (f32[160]{0:T(256)S(1)}, f32[160]{0:T(256)}, u32[]{:S(2)}) copy-start(f32[160]{0:T(256)} %param.16) | copy-start | bytes 1924
  51.3 4.3 %copy-start = (bf16[2,44,256,256]{3,2,1,0:T(8,128)(2,1)S(1)}, bf16[2,44,256,256]{3,2,1,0:T(8,128)(2,1)}, u32[]{:S(2)}) copy-start(bf16[2,44,256,256]{3,2,1,0:T(8,128)(2,1)} %pad.29.refs_1_) | copy-start | bytes 34603012
  69.1 7.0 %copy-start.5 = (f32[640]{0:T(1024)S(1)}, f32[640]{0:T(1024)}, u32[]{:S(2)}) copy-start(f32[640]{0:T(1024)} %param.20) | copy-start | bytes 7684
  69.1 7.1 %copy-start.6 = (f32[640]{0:T(1024)S(1)}, f32[640]{0:T(1024)}, u32[]{:S(2)}) copy-start(f32[640]{0:T(1024)} %param.23) | copy-start | bytes 7684
  70.1 30.0 %all-to-all-start.1 = ((bf16[8,256,160]{1,2,0:T(8,128)(2,1)}), bf16[8,256,160]{1,2,0:T(8,128)(2,1)S(1)}, u32[]{:S(2)}, u32[]{:S(2)}) async-start(bf16[8,256,160]{1,2,0:T(8,128)(2,1)} %copy.76), calls=%async_computation.1 | async-start | bytes 1310720 | tf_op jit(solution)/shard_map/all_to_all | solution.py:276
  100.8 0.7 copy-start.10
  100.8 0.7 copy-start.11
  107.0 3.8 %copy-start.7 = (s32[2,5]{1,0:T(2,128)S(1)}, s32[2,5]{1,0:T(2,128)}, u32[]{:S(2)}) copy-start(s32[2,5]{1,0:T(2,128)} %param.26) | copy-start | bytes 124
  107.0 35.0 %copy-start.9 = (s32[4]{0:T(128)S(1)}, s32[4]{0:T(128)}, u32[]{:S(2)}) copy-start(s32[4]{0:T(128)} %param.27) | copy-start | bytes 52
  107.0 36.6 %all-to-all-start.2 = ((bf16[256,8,240]{0,2,1:T(8,128)(2,1)}), bf16[256,8,240]{0,2,1:T(8,128)(2,1)S(1)}, u32[]{:S(2)}, u32[]{:S(2)}) async-start(bf16[256,8,240]{0,2,1:T(8,128)(2,1)} %bitcast.45), calls=%async_computation.2 | async-start | bytes 1966080 | tf_op jit(solution)/shard_map/all_to_all | solution.py:288
  143.6 0.9 copy-start.2
  147.6 29.8 %copy-start.4 = (f32[1280]{0:T(1024)S(1)}, f32[1280]{0:T(1024)}, u32[]{:S(2)}) copy-start(f32[1280]{0:T(1024)} %param.25) | copy-start | bytes 15364
Sparse Core Ops, SparseCore 0:
  12.6 87.6 all-gather.2

commit v2 on v1

--- a/solution.py
+++ b/solution.py
@@ -134,6 +134,28 @@
 STEP = 4
 
 
+def expand_kernel(taps, width, shift, steps, k_ref, o_ref):
+    inner = PHASES * width
+    for step in range(steps):
+        columns = []
+        for phase in range(PHASES):
+            begin = step * PHASES - phase - shift
+            low = min(max(begin, 0), taps)
+            high = min(max(begin + PHASES, 0), taps)
+            pieces = []
+            if low > begin and high > low:
+                pieces.append(jnp.zeros(((low - begin) * width, width), jnp.bfloat16))
+            if high > low:
+                pieces.append(k_ref[0, low * width : high * width, :])
+            missing = inner - sum(piece.shape[0] for piece in pieces)
+            if missing:
+                pieces.append(jnp.zeros((missing, width), jnp.bfloat16))
+            columns.append(pieces[0] if len(pieces) == 1 else jnp.concatenate(pieces, axis=0))
+        columns.append(jnp.zeros((inner, LANES - inner), jnp.bfloat16))
+        o_ref[0, step, :inner, :] = jnp.concatenate(columns, axis=1)
+        o_ref[0, step, inner:, :] = jnp.zeros((LANES - inner, LANES), jnp.bfloat16)
+
+
 def conv_kernel(rows, steps, x_ref, w_ref, o_ref):
     o_ref[0] = jnp.zeros_like(o_ref[0])
 
@@ -167,18 +189,15 @@
     spread = spread.transpose(2, 0, 1, 3).reshape(groups, total_rows, inner)
     spread = jnp.pad(spread, ((0, 0), (0, 0), (0, LANES - inner))).astype(jnp.float32)
     kernels = position_kernel.reshape(groups, width, width, taps).transpose(0, 3, 2, 1)
-    span = steps * PHASES
-    matrix = jnp.concatenate(
-        [
-            jnp.pad(
-                kernels,
-                ((0, 0), (shift + phase, span - taps - shift - phase), (0, 0), (0, 0)),
-            )
-            for phase in range(PHASES)
-        ],
-        axis=3,
-    ).reshape(groups, steps, inner, inner)
-    matrix = jnp.pad(matrix, ((0, 0), (0, 0), (0, LANES - inner), (0, LANES - inner)))
+    kernels = kernels.reshape(groups, taps * width, width)
+    matrix = pl.pallas_call(
+        lambda *refs: expand_kernel(taps, width, shift, steps, *refs),
+        out_shape=jax.ShapeDtypeStruct((groups, steps, LANES, LANES), jnp.bfloat16),
+        grid=(groups,),
+        in_specs=[pl.BlockSpec((1, taps * width, width), lambda g: (g, 0, 0))],
+        out_specs=pl.BlockSpec((1, steps, LANES, LANES), lambda g: (g, 0, 0, 0)),
+        compiler_params=pltpu.CompilerParams(vmem_limit_bytes=40 * 1024 * 1024),
+    )(kernels)
     response = pl.pallas_call(
         lambda *refs: conv_kernel(rows_padded, steps, *refs),
         out_shape=jax.ShapeDtypeStruct((groups, rows_padded, LANES), jnp.float32),
@@ -196,47 +215,53 @@
     return position[:, :frames].transpose(1, 0, 2).reshape(frames, channels)
 
 
+PER_STEP = 2
+
+
 def attention_kernel(listed, scale, ids_ref, mask_ref, q_ref, k_ref, v_ref, o_ref):
-    row = pl.program_id(0)
-    queries = q_ref[...]
-    scores, values = [], []
-    for at in range(listed):
-        begin = pl.multiple_of(ids_ref[row, at] * BLOCK, BLOCK)
-        score = lax.dot_general(
-            queries,
-            k_ref[pl.ds(begin, BLOCK), :],
-            (((1,), (1,)), ((), ())),
-            preferred_element_type=jnp.float32,
-        )
-        scores.append(jnp.where(mask_ref[row, at] > 0, score * scale, -jnp.inf))
-        values.append(v_ref[pl.ds(begin, BLOCK), :])
-    peak = scores[0]
-    for score in scores[1:]:
-        peak = jnp.maximum(peak, score)
-    peak = jnp.max(peak, axis=1, keepdims=True)
-    weights = [jnp.exp(score - peak) for score in scores]
-    total = weights[0]
-    for weight in weights[1:]:
-        total = total + weight
-    total = jnp.sum(total, axis=1, keepdims=True)
-    probability = jnp.concatenate([weight.astype(jnp.bfloat16) for weight in weights], axis=1)
-    context = jnp.dot(
-        probability, jnp.concatenate(values, axis=0), preferred_element_type=jnp.float32
-    )
-    o_ref[...] = (context / total).astype(jnp.bfloat16)
+    for place in range(PER_STEP):
+        row = pl.program_id(0) * PER_STEP + place
+        queries = q_ref[place * BLOCK : (place + 1) * BLOCK, :]
+        scores, values = [], []
+        for at in range(listed):
+            begin = pl.multiple_of(ids_ref[row, at] * BLOCK, BLOCK)
+            score = lax.dot_general(
+                queries,
+                k_ref[pl.ds(begin, BLOCK), :],
+                (((1,), (1,)), ((), ())),
+                preferred_element_type=jnp.float32,
+            )
+            scores.append(jnp.where(mask_ref[row, at] > 0, score * scale, -jnp.inf))
+            values.append(v_ref[pl.ds(begin, BLOCK), :])
+        peak = scores[0]
+        for score in scores[1:]:
+            peak = jnp.maximum(peak, score)
+        peak = jnp.max(peak, axis=1, keepdims=True)
+        weights = [jnp.exp(score - peak) for score in scores]
+        total = weights[0]
+        for weight in weights[1:]:
+            total = total + weight
+        total = jnp.sum(total, axis=1, keepdims=True)
+        probability = jnp.concatenate(
+            [weight.astype(jnp.bfloat16) for weight in weights], axis=1
+        )
+        context = jnp.dot(
+            probability, jnp.concatenate(values, axis=0), preferred_element_type=jnp.float32
+        )
+        o_ref[place * BLOCK : (place + 1) * BLOCK, :] = (context / total).astype(jnp.bfloat16)
 
 
 def attend_head(queries, keys, values, block_ids, allowed):
     frames, width = queries.shape
     blocks, listed = block_ids.shape
     whole = pl.BlockSpec((frames, width), lambda b, *_: (0, 0))
-    tile = pl.BlockSpec((BLOCK, width), lambda b, *_: (b, 0))
+    tile = pl.BlockSpec((PER_STEP * BLOCK, width), lambda b, *_: (b, 0))
     return pl.pallas_call(
         lambda *refs: attention_kernel(listed, 1.0 / math.sqrt(HEAD), *refs),
         out_shape=jax.ShapeDtypeStruct((frames, width), jnp.bfloat16),
         grid_spec=pltpu.PrefetchScalarGridSpec(
             num_scalar_prefetch=2,
-            grid=(blocks,),
+            grid=(blocks // PER_STEP,),
             in_specs=[tile, whole, whole],
             out_specs=tile,
         ),
@@ -261,16 +286,18 @@
 ):
     records = lax.axis_size("rec")
     record = lax.axis_index("rec")
-    share = query_weight.shape[0]
-    part = share // records
+    part = query_weight.shape[0] // records
     inner = HEADS * HEAD
-    stacked = jnp.stack((query_weight, key_weight, value_weight), axis=1)
-    stacked = stacked.reshape(share, 3, HEADS, HEAD).transpose(0, 2, 1, 3)
-    stacked = jnp.concatenate((stacked.reshape(share, 3 * inner), output_weight.T), axis=1)
-    mine = lax.dynamic_slice_in_dim(stacked, record * part, part, axis=0)
-
+    rows = [
+        lax.dynamic_slice_in_dim(weight, record * part, part, axis=0)
+        for weight in (query_weight, key_weight, value_weight)
+    ]
+    rows = jnp.stack(rows, axis=1).reshape(part, 3, HEADS, HEAD).transpose(0, 2, 1, 3)
+    output_rows = lax.dynamic_slice_in_dim(output_weight, record * part, part, axis=1).T
     incoming = lax.all_to_all(signal, "tm", split_axis=1, concat_axis=0, tiled=True)
-    weights = lax.all_gather(mine, ("tm", "rec"), axis=0, tiled=True)
+    weights = lax.all_gather(rows.reshape(part, 3 * inner), ("tm", "rec"), axis=0, tiled=True)
+    output_rows, incoming = lax.optimization_barrier((output_rows, incoming))
+    output_weights = lax.all_gather(output_rows, ("tm", "rec"), axis=0, tiled=True)
     listed = lax.all_gather(key_blocks, "tm", axis=0, tiled=True)
     position = position_term(incoming, position_kernel, position_bias)
     returned = lax.all_to_all(position, "tm", split_axis=0, concat_axis=1, tiled=True)
@@ -283,7 +310,7 @@
     )
     biases = jnp.stack((query_bias, jnp.zeros_like(query_bias), value_bias))
     biases = biases.reshape(3, HEADS, HEAD).transpose(1, 0, 2).reshape(-1)
-    projected = jnp.dot(normed, weights[:, : 3 * inner], preferred_element_type=jnp.float32)
+    projected = jnp.dot(normed, weights, preferred_element_type=jnp.float32)
     projected = (projected + biases).astype(jnp.bfloat16)
     headed = lax.all_to_all(projected, "tm", split_axis=1, concat_axis=0, tiled=True)
     blocks = listed.shape[0]
@@ -303,7 +330,7 @@
     context = lax.all_to_all(context, "tm", split_axis=0, concat_axis=1, tiled=True)
     projected = lax.dot_general(
         context,
-        weights[:, 3 * inner :],
+        output_weights,
         (((1,), (1,)), ((), ())),
         preferred_element_type=jnp.float32,
     )

time: 189 us -> 180 us (0.952)
  other arithmetic: 18.3 us -> 5.38 us
  blocking collectives: 45.2 us -> 32.3 us
  waiting for transfers between devices: 23.7 us -> 36.4 us
  starting transfers between devices: 17.1 us -> 21.4 us
  Pallas kernels: 23 us -> 26.6 us
  local copies, waits for them, and re-layouts: 39.3 us -> 36.3 us
    all_to_all x1 -> x0, blocking collectives: 14 us -> none  [by_heads(): lax.all_to_all(context, 'tm', split_axis=0, concat_axis=1, tiled=True)]
    concatenate x2 -> x0, other arithmetic: 12.8 us -> none  [the longest x1 11.6 us: position_term(): jnp.concatenate([jnp.pad(kernels, ((0, 0), (shift + phase, span - taps -...]
    all_to_all x0 -> x1, waiting for transfers between devices: none -> 8.64 us  [by_heads(): lax.all_to_all(context, 'tm', split_axis=0, concat_axis=1, tiled=True)]
    all_to_all x0 -> x1, starting transfers between devices: none -> 6.19 us  [by_heads(): lax.all_to_all(context, 'tm', split_axis=0, concat_axis=1, tiled=True)]
    pallas_call x0 -> x1, Pallas kernels: none -> 5.75 us  [position_term(): pl.pallas_call(lambda *refs: expand_kernel(taps, width, shift, steps, *re...]
    pad x1 -> x0, local copies, waits for them, and re-layouts: 5.64 us -> none  [position_term(): jnp.pad(matrix, ((0, 0), (0, 0), (0, LANES - inner), (0, LANES - inner)))]
    another operation x3, local copies, waits for them, and re-layouts: 3.34 us -> 0.36 us  [by_heads(): jnp.stack(rows, axis=1).reshape(part, 3, HEADS, HEAD).transpose(0, 2, 1, 3)]
    unnamed x29 -> x30, local copies, waits for them, and re-layouts: 7.6 us -> 9.8 us
  transfers between devices with their start and end apart: 4 -> 6, of which waited for: 1 -> 4; matrix products, arithmetic and copies ran while one was open for 22% -> 20% of each run, Pallas kernels for 4% -> 15%
where the time goes in v2:
time: 180 us; the launch traced here: 179 us
  waiting for transfers between devices  36.4 us (20%)
  local copies, waits for them, and re-layouts  36.3 us (20%)
  blocking collectives  32.3 us (18%)
  Pallas kernels  26.6 us (15%)
  starting transfers between devices  21.4 us (12%)
  between operations  13.7 us (8%)
  matrix products  7.15 us (4%)
  other arithmetic  5.38 us (3%)
    all_gather x1, blocking collectives, by_heads(): listed = lax.all_gather(key_blocks, 'tm', axis=0, tiled=True)  32.3 us
    all_to_all x1, waiting for transfers between devices, by_heads(): lax.all_to_all(position, 'tm', split_axis=0, concat_axis=1, tiled=True)  25.2 us
    pallas_call x1, Pallas kernels, attend_head(): pl.pallas_call(lambda *refs: attention_kernel(listed, 1.0 / math.sqrt(HEA...  12.4 us
    unnamed x30, local copies, waits for them, and re-layouts  9.8 us
    all_to_all x1, waiting for transfers between devices, by_heads(): lax.all_to_all(context, 'tm', split_axis=0, concat_axis=1, tiled=True)  8.64 us
    reshape x1, local copies, waits for them, and re-layouts, position_term(): position_kernel.reshape(groups, width, width, taps).transpose(0, 3, 2, 1)  8.63 us
    pallas_call x1, Pallas kernels, position_term(): pl.pallas_call(lambda *refs: conv_kernel(rows_padded, steps, *refs), out_...  8.44 us
    all_to_all x1, starting transfers between devices, by_heads(): lax.all_to_all(signal, 'tm', split_axis=1, concat_axis=0, tiled=True)  7.28 us
  transfers between devices with their start and end apart: 6, of which 4 were waited for; matrix products, arithmetic and copies ran while one was open for 20% of the time, Pallas kernels for 15%

profile of v2, /device:TPU:0, one launch (start us, length us, event | category | flops | bytes accessed | tf_op | source)
XLA Modules:
  0.0 179.3 jit_solution(1412734394692579460)
XLA Ops:
  6.5 0.9 constant_dynamic-slice_fusion
  8.2 1.0 reshape.77
  9.2 1.1 copy.70
  10.3 7.3 %all-to-all-start = ((bf16[256,8,160]{0,2,1:T(8,128)(2,1)}), bf16[256,8,160]{0,2,1:T(8,128)(2,1)S(1)}, u32[]{:S(2)}, u32[]{:S(2)}) async-start(bf16[256,8,160]{0,2,1:T(8,128)(2,1)} %bitcast.1), calls=%async_computation | async-start | bytes 1310720 | tf_op jit(solution)/shard_map/all_to_all | solution.py:297
  17.5 8.6 %copy.75 = bf16[2,80,80,128]{1,2,3,0:T(8,128)(2,1)} copy(bf16[2,80,80,128]{3,2,1,0:T(8,128)(2,1)} %bitcast.45) | data formatting | bytes 6553600 | tf_op jit(solution)/shard_map/reshape | solution.py:191
  26.2 2.5 %copy-done.2 = bf16[2,80,80,128]{1,2,3,0:T(8,128)(2,1)S(1)} copy-done((bf16[2,80,80,128]{1,2,3,0:T(8,128)(2,1)S(1)}, bf16[2,80,80,128]{1,2,3,0:T(8,128)(2,1)}, u32[]{:S(2)}) %copy-start.2) | copy-done | bytes 3276824
  28.7 5.8 %shard_map.136.refs_1_ = bf16[2,44,256,256]{3,2,1,0:T(8,128)(2,1)} custom-call(bf16[2,10240,80]{2,1,0:T(8,128)(2,1)S(1)} %bitcast.39), custom_call_target="tpu_custom_call" | custom-call | tf_op jit(solution)/shard_map/pallas_call | solution.py:193
  34.6 1.4 dynamic-slice_bitcast_fusion
  36.0 2.1 %all-to-all-done = bf16[256,8,160]{0,2,1:T(8,128)(2,1)S(1)} async-done(((bf16[256,8,160]{0,2,1:T(8,128)(2,1)}), bf16[256,8,160]{0,2,1:T(8,128)(2,1)S(1)}, u32[]{:S(2)}, u32[]{:S(2)}) %all-to-all-start) | async-done | bytes 655392 | tf_op jit(solution)/shard_map/all_to_all | solution.py:297
  39.0 0.6 reshape.72
  39.7 2.5 %copy.73 = bf16[2,736,3,80]{1,3,2,0:T(8,128)(2,1)S(1)} copy(bf16[2,736,3,80]{3,0,2,1:T(2,128)(2,1)S(1)} %bitcast.42) | data formatting | bytes 1413120 | tf_op jit(solution)/shard_map/transpose | solution.py:189
  42.6 4.3 %copy-done.1 = bf16[2,44,256,256]{3,2,1,0:T(8,128)(2,1)S(1)} copy-done((bf16[2,44,256,256]{3,2,1,0:T(8,128)(2,1)S(1)}, bf16[2,44,256,256]{3,2,1,0:T(8,128)(2,1)}, u32[]{:S(2)}) %copy-start.1) | copy-done | bytes 11534360
  46.9 8.4 %shard_map.137 = f32[2,688,256]{2,1,0:T(8,128)S(1)} custom-call(f32[2,736,256]{2,1,0:T(8,128)S(1)} %pad_convert_fusion.refs_0_, bf16[2,44,256,256]{3,2,1,0:T(8,128)(2,1)S(1)} %copy-done.1), custom_call_target="tpu_custom_call" | custom-call | tf_op jit(solution)/shard_map/pallas_call | solution.py:201
  55.3 3.1 %fusion.5 = bf16[2,683,240]{2,1,0:T(8,128)(2,1)S(1)} fusion(f32[2,688,256]{2,1,0:T(8,128)S(1)} %shard_map.137, f32[2,240]{1,0:T(2,128)S(1)} %tile.12), kind=kLoop, calls=%fused_computation.8 | loop fusion | flops 21637440 | bytes 1968960 | tf_op jit(solution)/shard_map/convert_element_type | solution.py:214
  58.4 1.3 reshape.76
  60.5 1.0 copy.77
  61.4 4.2 %all-to-all-start.1 = ((bf16[8,256,160]{1,2,0:T(8,128)(2,1)}), bf16[8,256,160]{1,2,0:T(8,128)(2,1)S(1)}, u32[]{:S(2)}, u32[]{:S(2)}) async-start(bf16[8,256,160]{1,2,0:T(8,128)(2,1)} %copy.77), calls=%async_computation.1 | async-start | bytes 1310720 | tf_op jit(solution)/shard_map/all_to_all | solution.py:303
  66.4 25.2 %all-to-all-done.1 = bf16[8,256,160]{1,2,0:T(8,128)(2,1)S(1)} async-done(((bf16[8,256,160]{1,2,0:T(8,128)(2,1)}), bf16[8,256,160]{1,2,0:T(8,128)(2,1)S(1)}, u32[]{:S(2)}, u32[]{:S(2)}) %all-to-all-start.1) | async-done | bytes 655392 | tf_op jit(solution)/shard_map/all_to_all | solution.py:303
  93.1 4.1 %fusion.1 = bf16[256,1920]{1,0:T(8,128)(2,1)S(1)} fusion(bf16[1280,1920]{1,0:T(8,128)(2,1)} %all-gather.4.cloned.1.call-done, f32[1920]{0:T(1024)S(1)} %add.69, f32[1280]{0:T(1024)S(1)} %copy-done.11, f32[1280]{0:T(1024)S(1)} %copy-done.12, f32[256]{0:T(256)S(1)} %add_rsqrt_fusion, f32[256]{0:T(256)S(1)} %broadcast_multiply_fusion, ...), kind=kOutput, calls=%fused_computation.3 | convolution fusion | flops 1261568000 | bytes 7884288 | tf_op jit(solution)/shard_map/dot_general | solution.py:313
  97.2 1.4 copy.82
  98.6 3.7 %all-to-all-start.2 = ((bf16[256,8,240]{0,2,1:T(8,128)(2,1)}), bf16[256,8,240]{0,2,1:T(8,128)(2,1)S(1)}, u32[]{:S(2)}, u32[]{:S(2)}) async-start(bf16[256,8,240]{0,2,1:T(8,128)(2,1)} %bitcast.44), calls=%async_computation.2 | async-start | bytes 1966080 | tf_op jit(solution)/shard_map/all_to_all | solution.py:315
  102.3 32.3 %all-gather = s32[8,2,5]{2,1,0:T(2,128)S(1)} all-gather(s32[1,2,5]{2,1,0:T(2,128)S(1)} %bitcast.56), channel_id=1, replica_groups=mesh['rec'=4,'tm'=8] {'tm'}, dimensions={0}, use_global_device_ids=true | all-gather | bytes 360 | tf_op jit(solution)/shard_map/all_gather | solution.py:301
  134.9 0.7 add_convert_fusion.2.refs_1_
  135.6 0.6 pad_add_fusion.refs_0_
  136.2 1.0 copy-done.4
  137.1 1.5 copy.83
  138.6 1.5 fusion.18
  140.2 12.4 %shard_map.138 = bf16[2048,80]{1,0:T(8,128)(2,1)} custom-call(s32[16,9]{1,0:T(8,128)} %pad_add_fusion.refs_0_, s32[16,9]{1,0:T(8,128)} %add_convert_fusion.2.refs_1_, bf16[2048,80]{1,0:T(8,128)(2,1)} %get-tuple-element.11.refs_2_, bf16[2048,80]{1,0:T(8,128)(2,1)} %get-tuple-element.10.refs_3_, bf16[2048,80]{1,0:T(8,128)(2,1)} %get-tuple-element.9.refs_4_), custom_call_target="tpu_custom_call" | custom-call | tf_op jit(solution)/shard_map/pallas_call | solution.py:259
  152.6 2.0 %copy.84 = bf16[8,256,80]{1,2,0:T(8,128)(2,1)} copy(bf16[8,256,80]{2,1,0:T(8,128)(2,1)} %bitcast.51) | data formatting | bytes 655360 | tf_op jit(solution)/shard_map/all_to_all | solution.py:330
  154.6 6.2 %all-to-all-start.3 = ((bf16[8,256,80]{1,2,0:T(8,128)(2,1)}), bf16[8,256,80]{1,2,0:T(8,128)(2,1)S(1)}, u32[]{:S(2)}, u32[]{:S(2)}) async-start(bf16[8,256,80]{1,2,0:T(8,128)(2,1)} %copy.84), calls=%async_computation.3 | async-start | bytes 655360 | tf_op jit(solution)/shard_map/all_to_all | solution.py:330
  160.8 8.6 %all-to-all-done.3 = bf16[8,256,80]{1,2,0:T(8,128)(2,1)S(1)} async-done(((bf16[8,256,80]{1,2,0:T(8,128)(2,1)}), bf16[8,256,80]{1,2,0:T(8,128)(2,1)S(1)}, u32[]{:S(2)}, u32[]{:S(2)}) %all-to-all-start.3) | async-done | bytes 327712 | tf_op jit(solution)/shard_map/all_to_all | solution.py:330
  169.4 3.0 %fusion.2 = bf16[256,1280]{1,0:T(8,128)(2,1)} fusion(bf16[256,640]{0,1:T(8,128)(2,1)S(1)} %bitcast.52, bf16[1280,640]{1,0:T(8,128)(2,1)} %all-gather.6.cloned.1.call-done, f32[1280]{0:T(1024)S(1)} %copy-done.5, f32[256,1280]{1,0:T(8,128)S(1)} %copy.78, bf16[256,1280]{1,0:T(8,128)(2,1)S(1)} %copy-done.3), kind=kOutput, calls=%fused_computation.4 | convolution fusion | flops 421068800 | bytes 4592640 | tf_op jit(solution)/shard_map/dot_general | solution.py:331
  (65 shorter events, 5.3 us)
Async XLA Ops:
  6.5 1.2 copy-start
  6.5 2.6 %copy-start.3 = (bf16[256,1280]{1,0:T(8,128)(2,1)S(1)}, bf16[256,1280]{1,0:T(8,128)(2,1)}, u32[]{:S(2)}) copy-start(bf16[256,1280]{1,0:T(8,128)(2,1)} %param.14) | copy-start | bytes 1966084
  6.5 86.3 %all-gather.4.cloned.1.call-start = ((), (), s32[]{:S(2)}) async-start(), calls=%async_computation.4 | async-start | bytes 5068800 | tf_op jit(solution)/shard_map/all_gather | solution.py:298
  10.3 27.9 %all-to-all-start = ((bf16[256,8,160]{0,2,1:T(8,128)(2,1)}), bf16[256,8,160]{0,2,1:T(8,128)(2,1)S(1)}, u32[]{:S(2)}, u32[]{:S(2)}) async-start(bf16[256,8,160]{0,2,1:T(8,128)(2,1)} %bitcast.1), calls=%async_computation | async-start | bytes 1310720 | tf_op jit(solution)/shard_map/all_to_all | solution.py:297
  26.2 2.5 %copy-start.2 = (bf16[2,80,80,128]{1,2,3,0:T(8,128)(2,1)S(1)}, bf16[2,80,80,128]{1,2,3,0:T(8,128)(2,1)}, u32[]{:S(2)}) copy-start(bf16[2,80,80,128]{1,2,3,0:T(8,128)(2,1)} %copy.75) | copy-start | bytes 9830404
  28.7 5.8 %copy-start.9 = (f32[160]{0:T(256)S(1)}, f32[160]{0:T(256)}, u32[]{:S(2)}) copy-start(f32[160]{0:T(256)} %param.16) | copy-start | bytes 1924
  42.6 4.3 %copy-start.1 = (bf16[2,44,256,256]{3,2,1,0:T(8,128)(2,1)S(1)}, bf16[2,44,256,256]{3,2,1,0:T(8,128)(2,1)}, u32[]{:S(2)}) copy-start(bf16[2,44,256,256]{3,2,1,0:T(8,128)(2,1)} %shard_map.136.refs_1_) | copy-start | bytes 34603012
  60.4 5.2 %copy-start.6 = (f32[640]{0:T(1024)S(1)}, f32[640]{0:T(1024)}, u32[]{:S(2)}) copy-start(f32[640]{0:T(1024)} %param.20) | copy-start | bytes 7684
  60.5 5.3 %copy-start.7 = (f32[640]{0:T(1024)S(1)}, f32[640]{0:T(1024)}, u32[]{:S(2)}) copy-start(f32[640]{0:T(1024)} %param.23) | copy-start | bytes 7684
  61.4 30.2 %all-to-all-start.1 = ((bf16[8,256,160]{1,2,0:T(8,128)(2,1)}), bf16[8,256,160]{1,2,0:T(8,128)(2,1)S(1)}, u32[]{:S(2)}, u32[]{:S(2)}) async-start(bf16[8,256,160]{1,2,0:T(8,128)(2,1)} %copy.77), calls=%async_computation.1 | async-start | bytes 1310720 | tf_op jit(solution)/shard_map/all_to_all | solution.py:303
  65.6 95.1 %all-gather.6.cloned.1.call-start = ((), (), s32[]{:S(2)}) async-start(), calls=%async_computation.5 | async-start | bytes 1689600 | tf_op jit(solution)/shard_map/all_gather | solution.py:300
  92.4 0.7 copy-start.11
  92.4 0.7 copy-start.12
  98.5 3.7 %copy-start.8 = (s32[2,5]{1,0:T(2,128)S(1)}, s32[2,5]{1,0:T(2,128)}, u32[]{:S(2)}) copy-start(s32[2,5]{1,0:T(2,128)} %param.26) | copy-start | bytes 124
  98.5 36.1 %copy-start.10 = (s32[4]{0:T(128)S(1)}, s32[4]{0:T(128)}, u32[]{:S(2)}) copy-start(s32[4]{0:T(128)} %param.27) | copy-start | bytes 52
  98.6 37.6 %all-to-all-start.2 = ((bf16[256,8,240]{0,2,1:T(8,128)(2,1)}), bf16[256,8,240]{0,2,1:T(8,128)(2,1)S(1)}, u32[]{:S(2)}, u32[]{:S(2)}) async-start(bf16[256,8,240]{0,2,1:T(8,128)(2,1)} %bitcast.44), calls=%async_computation.2 | async-start | bytes 1966080 | tf_op jit(solution)/shard_map/all_to_all | solution.py:315
  136.2 1.0 copy-start.4
  140.1 29.3 %copy-start.5 = (f32[1280]{0:T(1024)S(1)}, f32[1280]{0:T(1024)}, u32[]{:S(2)}) copy-start(f32[1280]{0:T(1024)} %param.25) | copy-start | bytes 15364
  154.6 14.9 %all-to-all-start.3 = ((bf16[8,256,80]{1,2,0:T(8,128)(2,1)}), bf16[8,256,80]{1,2,0:T(8,128)(2,1)S(1)}, u32[]{:S(2)}, u32[]{:S(2)}) async-start(bf16[8,256,80]{1,2,0:T(8,128)(2,1)} %copy.84), calls=%async_computation.3 | async-start | bytes 655360 | tf_op jit(solution)/shard_map/all_to_all | solution.py:330
Sparse Core Ops, SparseCore 0:
  10.3 82.5 all-gather.3
  95.8 57.7 all-gather.5

commit v3 on v2

--- a/solution.py
+++ b/solution.py
@@ -156,8 +156,8 @@
         o_ref[0, step, inner:, :] = jnp.zeros((LANES - inner, LANES), jnp.bfloat16)
 
 
-def conv_kernel(rows, steps, x_ref, w_ref, o_ref):
-    o_ref[0] = jnp.zeros_like(o_ref[0])
+def conv_kernel(rows, steps, x_ref, w_ref, b_ref, o_ref, total_ref):
+    total_ref[...] = jnp.zeros_like(total_ref)
 
     for step in range(0, steps, STEP):
         window = jnp.concatenate(
@@ -168,7 +168,10 @@
             axis=1,
         )
         taps = w_ref[0, step : step + STEP].reshape(STEP * LANES, LANES)
-        o_ref[0] += jnp.dot(window, taps, preferred_element_type=jnp.float32)
+        total_ref[...] += jnp.dot(window, taps, preferred_element_type=jnp.float32)
+    value = total_ref[...] + b_ref[0]
+    gelu = value * (1.0 + lax.erf(value * (0.5**0.5))) * 0.5
+    o_ref[0] = gelu.astype(jnp.bfloat16)
 
 
 def position_term(incoming, position_kernel, position_bias):
@@ -196,26 +199,28 @@
         grid=(groups,),
         in_specs=[pl.BlockSpec((1, taps * width, width), lambda g: (g, 0, 0))],
         out_specs=pl.BlockSpec((1, steps, LANES, LANES), lambda g: (g, 0, 0, 0)),
-        compiler_params=pltpu.CompilerParams(vmem_limit_bytes=40 * 1024 * 1024),
+        compiler_params=pltpu.CompilerParams(vmem_limit_bytes=56 * 1024 * 1024),
     )(kernels)
-    response = pl.pallas_call(
+    biases = jnp.tile(position_bias.reshape(groups, 1, width), (1, 1, PHASES))
+    biases = jnp.pad(biases, ((0, 0), (0, 0), (0, LANES - inner)))
+    position = pl.pallas_call(
         lambda *refs: conv_kernel(rows_padded, steps, *refs),
-        out_shape=jax.ShapeDtypeStruct((groups, rows_padded, LANES), jnp.float32),
+        out_shape=jax.ShapeDtypeStruct((groups, rows_padded, LANES), jnp.bfloat16),
         grid=(groups,),
         in_specs=[
             pl.BlockSpec((1, total_rows, LANES), lambda g: (g, 0, 0)),
             pl.BlockSpec((1, steps, LANES, LANES), lambda g: (g, 0, 0, 0)),
+            pl.BlockSpec((1, 1, LANES), lambda g: (g, 0, 0)),
         ],
         out_specs=pl.BlockSpec((1, rows_padded, LANES), lambda g: (g, 0, 0)),
-        compiler_params=pltpu.CompilerParams(vmem_limit_bytes=40 * 1024 * 1024),
-    )(spread, matrix)
-    biases = jnp.tile(position_bias.reshape(groups, 1, width), (1, 1, PHASES))
-    position = jax.nn.gelu(response[:, :rows, :inner] + biases, approximate=False)
-    position = position.astype(jnp.bfloat16).reshape(groups, rows * PHASES, width)
+        scratch_shapes=[pltpu.VMEM((rows_padded, LANES), jnp.float32)],
+        compiler_params=pltpu.CompilerParams(vmem_limit_bytes=56 * 1024 * 1024),
+    )(spread, matrix, biases)
+    position = position[:, :rows, :inner].reshape(groups, rows * PHASES, width)
     return position[:, :frames].transpose(1, 0, 2).reshape(frames, channels)
 
 
-PER_STEP = 2
+PER_STEP = 4
 
 
 def attention_kernel(listed, scale, ids_ref, mask_ref, q_ref, k_ref, v_ref, o_ref):
@@ -298,9 +303,11 @@
     weights = lax.all_gather(rows.reshape(part, 3 * inner), ("tm", "rec"), axis=0, tiled=True)
     output_rows, incoming = lax.optimization_barrier((output_rows, incoming))
     output_weights = lax.all_gather(output_rows, ("tm", "rec"), axis=0, tiled=True)
-    listed = lax.all_gather(key_blocks, "tm", axis=0, tiled=True)
     position = position_term(incoming, position_kernel, position_bias)
+    own_list, position = lax.optimization_barrier((key_blocks, position))
+    listed = lax.all_gather(own_list, "tm", axis=0, tiled=True)
     returned = lax.all_to_all(position, "tm", split_axis=0, concat_axis=1, tiled=True)
+    returned, listed = lax.optimization_barrier((returned, listed))
     hidden = signal.astype(jnp.float32) + returned.astype(jnp.float32)
     average = jnp.mean(hidden, axis=-1, keepdims=True)
     centered = hidden - average

time: 180 us -> 174 us (0.967)
  local copies, waits for them, and re-layouts: 36.3 us -> 28.7 us
  Pallas kernels: 26.6 us -> 31.2 us
  waiting for transfers between devices: 36.4 us -> 34.3 us
  other arithmetic: 5.38 us -> 3.46 us
  blocking collectives: 32.3 us -> 34.2 us
    all_to_all x1, waiting for transfers between devices: 25.2 us -> 0.01 us  [by_heads(): lax.all_to_all(position, 'tm', split_axis=0, concat_axis=1, tiled=True)]
    all_to_all x1, waiting for transfers between devices: 0.01 us -> 22.4 us  [by_heads(): lax.all_to_all(projected, 'tm', split_axis=1, concat_axis=0, tiled=True)]
    unnamed x30 -> x22, local copies, waits for them, and re-layouts: 9.8 us -> 1.67 us
    pallas_call x1, Pallas kernels: 8.44 us -> 11.9 us  [position_term(): pl.pallas_call(lambda *refs: conv_kernel(rows_padded, steps, *refs), out_...]
    convert_element_type x2 -> x0, other arithmetic: 3.22 us -> none  [the longest x1 3.11 us: position_term(): position.astype(jnp.bfloat16).reshape(groups, rows * PHASES, width)]
    all_to_all x1, starting transfers between devices: 6.19 us -> 3.9 us  [by_heads(): lax.all_to_all(context, 'tm', split_axis=0, concat_axis=1, tiled=True)]
    all_gather x1, blocking collectives: 32.3 us -> 34.2 us  [by_heads(): listed = lax.all_gather(own_list, 'tm', axis=0, tiled=True)]
  transfers between devices with their start and end apart: 6 -> 6, of which waited for: 4 -> 4; matrix products, arithmetic and copies ran while one was open for 20% -> 19% of each run, Pallas kernels for 15% -> 18%
where the time goes in v3:
time: 174 us; the launch traced here: 173 us
  waiting for transfers between devices  34.3 us (20%)
  blocking collectives  34.2 us (20%)
  Pallas kernels  31.2 us (18%)
  local copies, waits for them, and re-layouts  28.7 us (16%)
  starting transfers between devices  20.1 us (12%)
  between operations  13.6 us (8%)
  matrix products  7.17 us (4%)
  other arithmetic  3.46 us (2%)
    all_gather x1, blocking collectives, by_heads(): listed = lax.all_gather(own_list, 'tm', axis=0, tiled=True)  34.2 us
    all_to_all x1, waiting for transfers between devices, by_heads(): lax.all_to_all(projected, 'tm', split_axis=1, concat_axis=0, tiled=True)  22.4 us
    pallas_call x1, Pallas kernels, position_term(): pl.pallas_call(lambda *refs: conv_kernel(rows_padded, steps, *refs), out_...  11.9 us
    pallas_call x1, Pallas kernels, attend_head(): pl.pallas_call(lambda *refs: attention_kernel(listed, 1.0 / math.sqrt(HEA...  11.8 us
    all_to_all x1, waiting for transfers between devices, by_heads(): lax.all_to_all(context, 'tm', split_axis=0, concat_axis=1, tiled=True)  9.06 us
    reshape x1, local copies, waits for them, and re-layouts, position_term(): position_kernel.reshape(groups, width, width, taps).transpose(0, 3, 2, 1)  8.6 us
    pallas_call x1, Pallas kernels, position_term(): pl.pallas_call(lambda *refs: expand_kernel(taps, width, shift, steps, *re...  7.51 us
    all_to_all x1, starting transfers between devices, by_heads(): lax.all_to_all(signal, 'tm', split_axis=1, concat_axis=0, tiled=True)  7.28 us
  transfers between devices with their start and end apart: 6, of which 4 were waited for; matrix products, arithmetic and copies ran while one was open for 19% of the time, Pallas kernels for 18%

profile of v3, /device:TPU:0, one launch (start us, length us, event | category | flops | bytes accessed | tf_op | source)
XLA Modules:
  0.0 172.9 jit_solution(17881479980825494953)
XLA Ops:
  6.5 0.9 constant_dynamic-slice_fusion
  8.2 1.0 reshape.77
  9.2 1.1 copy.74
  10.3 7.3 %all-to-all-start = ((bf16[256,8,160]{0,2,1:T(8,128)(2,1)}), bf16[256,8,160]{0,2,1:T(8,128)(2,1)S(1)}, u32[]{:S(2)}, u32[]{:S(2)}) async-start(bf16[256,8,160]{0,2,1:T(8,128)(2,1)} %bitcast.1), calls=%async_computation | async-start | bytes 1310720 | tf_op jit(solution)/shard_map/all_to_all | solution.py:302
  17.5 8.6 %copy.79 = bf16[2,80,80,128]{1,2,3,0:T(8,128)(2,1)} copy(bf16[2,80,80,128]{3,2,1,0:T(8,128)(2,1)} %bitcast.44) | data formatting | bytes 6553600 | tf_op jit(solution)/shard_map/reshape | solution.py:194
  26.1 7.5 %shard_map.136.refs_1_ = bf16[2,44,256,256]{3,2,1,0:T(8,128)(2,1)} custom-call(bf16[2,10240,80]{2,1,0:T(8,128)(2,1)} %bitcast.40), custom_call_target="tpu_custom_call" | custom-call | tf_op jit(solution)/shard_map/pallas_call | solution.py:196
  33.8 0.6 pad.14.refs_2_
  34.4 1.4 dynamic-slice_bitcast_fusion
  35.8 2.3 %all-to-all-done = bf16[256,8,160]{0,2,1:T(8,128)(2,1)S(1)} async-done(((bf16[256,8,160]{0,2,1:T(8,128)(2,1)}), bf16[256,8,160]{0,2,1:T(8,128)(2,1)S(1)}, u32[]{:S(2)}, u32[]{:S(2)}) %all-to-all-start) | async-done | bytes 655392 | tf_op jit(solution)/shard_map/all_to_all | solution.py:302
  38.2 0.5 copy.90
  39.0 0.6 reshape.71
  39.7 2.5 %copy.77 = bf16[2,736,3,80]{1,3,2,0:T(8,128)(2,1)S(1)} copy(bf16[2,736,3,80]{3,0,2,1:T(2,128)(2,1)S(1)} %bitcast.42) | data formatting | bytes 1413120 | tf_op jit(solution)/shard_map/transpose | solution.py:192
  42.5 1.3 pad_convert_fusion.refs_0_
  43.8 11.9 %shard_map.137 = bf16[2,688,256]{2,1,0:T(8,128)(2,1)} custom-call(f32[2,736,256]{2,1,0:T(8,128)} %pad_convert_fusion.refs_0_, bf16[2,44,256,256]{3,2,1,0:T(8,128)(2,1)} %shard_map.136.refs_1_, f32[2,1,256]{2,1,0:T(1,128)} %pad.14.refs_2_), custom_call_target="tpu_custom_call" | custom-call | tf_op jit(solution)/shard_map/pallas_call | solution.py:206
  55.7 2.4 %reshape.75 = bf16[2,2049,80]{2,1,0:T(8,128)(2,1)S(1)} reshape(bf16[2,683,240]{2,1,0:T(8,128)(2,1)} %bitcast.46) | data formatting | bytes 1311360 | tf_op jit(solution)/shard_map/reshape | solution.py:219
  58.1 0.5 copy.81
  58.7 0.9 copy.94
  59.6 3.8 %all-to-all-start.1 = ((bf16[8,256,160]{1,2,0:T(8,128)(2,1)}), bf16[8,256,160]{1,2,0:T(8,128)(2,1)S(1)}, u32[]{:S(2)}, u32[]{:S(2)}) async-start(bf16[8,256,160]{1,2,0:T(8,128)(2,1)} %bitcast.38), calls=%async_computation.1 | async-start | bytes 1310720 | tf_op jit(solution)/shard_map/all_to_all | solution.py:309
  64.2 34.2 %all-gather = s32[8,2,5]{2,1,0:T(2,128)S(1)} all-gather(s32[1,2,5]{2,1,0:T(2,128)S(1)} %bitcast.56), channel_id=1, replica_groups=mesh['rec'=4,'tm'=8] {'tm'}, dimensions={0}, use_global_device_ids=true | all-gather | bytes 360 | tf_op jit(solution)/shard_map/all_gather | solution.py:308
  99.4 4.1 %fusion.1 = bf16[256,1920]{1,0:T(8,128)(2,1)S(1)} fusion(bf16[1280,1920]{1,0:T(8,128)(2,1)} %all-gather.4.cloned.1.call-done, f32[1920]{0:T(1024)S(1)} %add.61, bf16[256,1280]{1,0:T(8,128)(2,1)S(1)} %copy.83, bf16[256,1280]{1,0:T(8,128)(2,1)S(1)} %copy-done.1, f32[1280]{0:T(1024)S(1)} %copy-done.7, f32[1280]{0:T(1024)S(1)} %copy-done.8, ...), kind=kOutput, calls=%fused_computation.3 | convolution fusion | flops 1261895680 | bytes 7228928 | tf_op jit(solution)/shard_map/dot_general | solution.py:320
  103.5 1.4 copy.87
  104.9 5.1 %all-to-all-start.2 = ((bf16[256,8,240]{0,2,1:T(8,128)(2,1)}), bf16[256,8,240]{0,2,1:T(8,128)(2,1)S(1)}, u32[]{:S(2)}, u32[]{:S(2)}) async-start(bf16[256,8,240]{0,2,1:T(8,128)(2,1)} %bitcast.16), calls=%async_computation.2 | async-start | bytes 1966080 | tf_op jit(solution)/shard_map/all_to_all | solution.py:322
  110.3 0.7 add_convert_fusion.2.refs_1_
  111.0 0.6 pad_add_fusion.refs_0_
  111.6 22.4 %all-to-all-done.2 = bf16[256,8,240]{0,2,1:T(8,128)(2,1)S(1)} async-done(((bf16[256,8,240]{0,2,1:T(8,128)(2,1)}), bf16[256,8,240]{0,2,1:T(8,128)(2,1)S(1)}, u32[]{:S(2)}, u32[]{:S(2)}) %all-to-all-start.2) | async-done | bytes 983072 | tf_op jit(solution)/shard_map/all_to_all | solution.py:322
  133.9 0.5 copy.88
  134.5 1.5 fusion.8
  136.0 11.8 %shard_map.138 = bf16[2048,80]{1,0:T(8,128)(2,1)} custom-call(s32[16,9]{1,0:T(8,128)} %pad_add_fusion.refs_0_, s32[16,9]{1,0:T(8,128)} %add_convert_fusion.2.refs_1_, bf16[2048,80]{1,0:T(8,128)(2,1)} %get-tuple-element.19.refs_2_, bf16[2048,80]{1,0:T(8,128)(2,1)} %get-tuple-element.18.refs_3_, bf16[2048,80]{1,0:T(8,128)(2,1)} %get-tuple-element.17.refs_4_), custom_call_target="tpu_custom_call" | custom-call | tf_op jit(solution)/shard_map/pallas_call | solution.py:264
  147.8 2.0 %copy.89 = bf16[8,256,80]{1,2,0:T(8,128)(2,1)} copy(bf16[8,256,80]{2,1,0:T(8,128)(2,1)} %bitcast.51) | data formatting | bytes 655360 | tf_op jit(solution)/shard_map/all_to_all | solution.py:337
  149.8 3.9 %all-to-all-start.3 = ((bf16[8,256,80]{1,2,0:T(8,128)(2,1)}), bf16[8,256,80]{1,2,0:T(8,128)(2,1)S(1)}, u32[]{:S(2)}, u32[]{:S(2)}) async-start(bf16[8,256,80]{1,2,0:T(8,128)(2,1)} %copy.89), calls=%async_computation.3 | async-start | bytes 655360 | tf_op jit(solution)/shard_map/all_to_all | solution.py:337
  153.9 9.1 %all-to-all-done.3 = bf16[8,256,80]{1,2,0:T(8,128)(2,1)S(1)} async-done(((bf16[8,256,80]{1,2,0:T(8,128)(2,1)}), bf16[8,256,80]{1,2,0:T(8,128)(2,1)S(1)}, u32[]{:S(2)}, u32[]{:S(2)}) %all-to-all-start.3) | async-done | bytes 327712 | tf_op jit(solution)/shard_map/all_to_all | solution.py:337
  163.0 3.0 %fusion.2 = bf16[256,1280]{1,0:T(8,128)(2,1)} fusion(bf16[256,640]{0,1:T(8,128)(2,1)S(1)} %bitcast.52, bf16[1280,640]{1,0:T(8,128)(2,1)} %all-gather.6.cloned.1.call-done, bf16[256,1280]{1,0:T(8,128)(2,1)S(1)} %copy.83, bf16[256,1280]{1,0:T(8,128)(2,1)S(1)} %copy-done.1, f32[1280]{0:T(1024)S(1)} %copy-done.9), kind=kOutput, calls=%fused_computation.4 | convolution fusion | flops 421396480 | bytes 3937280 | tf_op jit(solution)/shard_map/dot_general | solution.py:338
  (57 shorter events, 3.8 us)
Async XLA Ops:
  6.5 1.2 copy-start
  6.5 2.6 %copy-start.1 = (bf16[256,1280]{1,0:T(8,128)(2,1)S(1)}, bf16[256,1280]{1,0:T(8,128)(2,1)}, u32[]{:S(2)}) copy-start(bf16[256,1280]{1,0:T(8,128)(2,1)} %param.14) | copy-start | bytes 1966084
  6.5 92.8 %all-gather.4.cloned.1.call-start = ((), (), s32[]{:S(2)}) async-start(), calls=%async_computation.4 | async-start | bytes 5068800 | tf_op jit(solution)/shard_map/all_gather | solution.py:303
  10.3 27.9 %all-to-all-start = ((bf16[256,8,160]{0,2,1:T(8,128)(2,1)}), bf16[256,8,160]{0,2,1:T(8,128)(2,1)S(1)}, u32[]{:S(2)}, u32[]{:S(2)}) async-start(bf16[256,8,160]{0,2,1:T(8,128)(2,1)} %bitcast.1), calls=%async_computation | async-start | bytes 1310720 | tf_op jit(solution)/shard_map/all_to_all | solution.py:302
  26.1 7.5 %copy-start.5 = (f32[160]{0:T(256)S(1)}, f32[160]{0:T(256)}, u32[]{:S(2)}) copy-start(f32[160]{0:T(256)} %param.16) | copy-start | bytes 1924
  58.6 4.8 %copy-start.2 = (f32[640]{0:T(1024)S(1)}, f32[640]{0:T(1024)}, u32[]{:S(2)}) copy-start(f32[640]{0:T(1024)} %param.20) | copy-start | bytes 7684
  58.7 4.9 %copy-start.3 = (f32[640]{0:T(1024)S(1)}, f32[640]{0:T(1024)}, u32[]{:S(2)}) copy-start(f32[640]{0:T(1024)} %param.23) | copy-start | bytes 7684
  58.7 5.5 %copy-start.4 = (s32[2,5]{1,0:T(2,128)S(1)}, s32[2,5]{1,0:T(2,128)}, u32[]{:S(2)}) copy-start(s32[2,5]{1,0:T(2,128)} %param.26) | copy-start | bytes 124
  59.6 38.8 %all-to-all-start.1 = ((bf16[8,256,160]{1,2,0:T(8,128)(2,1)}), bf16[8,256,160]{1,2,0:T(8,128)(2,1)S(1)}, u32[]{:S(2)}, u32[]{:S(2)}) async-start(bf16[8,256,160]{1,2,0:T(8,128)(2,1)} %bitcast.38), calls=%async_computation.1 | async-start | bytes 1310720 | tf_op jit(solution)/shard_map/all_to_all | solution.py:309
  63.4 90.5 %all-gather.6.cloned.1.call-start = ((), (), s32[]{:S(2)}) async-start(), calls=%async_computation.5 | async-start | bytes 1689600 | tf_op jit(solution)/shard_map/all_gather | solution.py:305
  98.6 0.7 copy-start.7
  98.7 0.7 copy-start.8
  104.9 5.1 %copy-start.6 = (s32[4]{0:T(128)S(1)}, s32[4]{0:T(128)}, u32[]{:S(2)}) copy-start(s32[4]{0:T(128)} %param.27) | copy-start | bytes 52
  104.9 29.1 %all-to-all-start.2 = ((bf16[256,8,240]{0,2,1:T(8,128)(2,1)}), bf16[256,8,240]{0,2,1:T(8,128)(2,1)S(1)}, u32[]{:S(2)}, u32[]{:S(2)}) async-start(bf16[256,8,240]{0,2,1:T(8,128)(2,1)} %bitcast.16), calls=%async_computation.2 | async-start | bytes 1966080 | tf_op jit(solution)/shard_map/all_to_all | solution.py:322
  136.0 27.0 %copy-start.9 = (f32[1280]{0:T(1024)S(1)}, f32[1280]{0:T(1024)}, u32[]{:S(2)}) copy-start(f32[1280]{0:T(1024)} %param.25) | copy-start | bytes 15364
  149.8 13.2 %all-to-all-start.3 = ((bf16[8,256,80]{1,2,0:T(8,128)(2,1)}), bf16[8,256,80]{1,2,0:T(8,128)(2,1)S(1)}, u32[]{:S(2)}, u32[]{:S(2)}) async-start(bf16[8,256,80]{1,2,0:T(8,128)(2,1)} %copy.89), calls=%async_computation.3 | async-start | bytes 655360 | tf_op jit(solution)/shard_map/all_to_all | solution.py:337
Sparse Core Ops, SparseCore 0:
  10.3 82.4 all-gather.3
  95.7 58.1 all-gather.5
